TPU v7x, 32 devices: a whole 2x2x4 slice. The times are simulated.
32 devices in a mesh: section: 2 (over y), expert: 16 (over z, x, core).
Axes of the slice: x: 2, y: 2, z: 4, core: 2. Of those that a mesh axis runs over, the one named last changes fastest.
Arguments:
- inputs: bfloat16 [2, 256, 2560], P('section', 'expert'), may hold values from -6 to 6
- norm_gain: float32 [2, 2, 2560], P(None, 'section'), may hold values from 0.5 to 1.5
- router: bfloat16 [2, 2, 2560, 16], P(None, 'section'), may hold values from -0.125 to 0.125
- w_gate: bfloat16 [2, 2, 16, 2560, 768], P(None, 'section', 'expert'), may hold values from -0.125 to 0.125
- w_up: bfloat16 [2, 2, 16, 2560, 768], P(None, 'section', 'expert'), may hold values from -0.125 to 0.125
- w_down: bfloat16 [2, 2, 16, 768, 2560], P(None, 'section', 'expert'), may hold values from -0.21875 to 0.21875
- routes: int32 [2, 2, 2, 256, 6], P(None, 'section'), may hold values from 0 to 15, all different within a row; in each aligned block of 16 rows (0 to 15, 16 to 31, ..., all dimensions but the last counted through in order) at most 9 rows name the same one
Outputs:
- outputs: bfloat16 [2, 256, 2560], P('section', 'expert')
Inputs may be any that keep to these rules, and one draw needn't show every extreme that they name: Each row names 6 different experts. In each aligned block of 16 rows of routes (the tokens of one index of expert in one micro-batch at one layer), no expert is named by more than 9 rows.
All inputs are finite; a program needn't handle non-finite values.
Results may differ from a plain program's by a relative error of at most 0.012.
Values may be sent and summed in bfloat16 or wider, within the bound.
A program may use at most 64 MiB of HBM per device.

v0:
```python
import jax
import jax.numpy as jnp
from jax import lax
from jax.sharding import PartitionSpec as P


def passed_along(array, axis, by):
    size = lax.axis_size(axis)
    return lax.ppermute(array, axis, [(i, (i + by) % size) for i in range(size)])


def passed_along_2(block, axis, distance):
    devices = range(lax.axis_size(axis))
    route = [(i - distance, i) for i in devices if i - distance in devices]
    return lax.ppermute(block, axis, route)


def normalize(values, gain_row):
    wide = values.astype(jnp.float32)
    scale = lax.rsqrt(jnp.mean(wide * wide, axis=-1, keepdims=True) + 1e-06)
    return (wide * scale * gain_row).astype(jnp.bfloat16)


def gate_weights(normed, router_now, routes_rows):
    scores = jnp.dot(normed, router_now, preferred_element_type=jnp.float32)
    expert_ids = lax.broadcasted_iota(jnp.int32, (1, 1, router_now.shape[1]), 2)
    onehot = (routes_rows[:, :, None] == expert_ids).astype(jnp.float32)
    picked = jnp.sum(onehot * scores[:, None, :], axis=2)
    sigmoid_of = jax.nn.sigmoid(picked)
    return sigmoid_of / jnp.sum(sigmoid_of, axis=1, keepdims=True)


def slot_table(routes_rows, slab_rows, experts):
    top_k = routes_rows.shape[1]
    blocks = routes_rows.reshape(-1, slab_rows * top_k)
    expert_ids = lax.broadcasted_iota(jnp.int32, (1, 1, experts), 2)
    onehot = (blocks[:, :, None] == expert_ids).astype(jnp.int32)
    before = jnp.cumsum(onehot, axis=1) - onehot
    return jnp.sum(before * onehot, axis=2).reshape(routes_rows.shape)


def expert_rows(rows_in, gate_mat, up_mat, down_mat):
    gate_proj = jnp.dot(rows_in, gate_mat, preferred_element_type=jnp.float32)
    up_proj = jnp.dot(rows_in, up_mat, preferred_element_type=jnp.float32)
    hidden = (jax.nn.silu(gate_proj) * up_proj).astype(jnp.bfloat16)
    return jnp.dot(hidden, down_mat, preferred_element_type=jnp.float32).astype(jnp.bfloat16)


def weighted_rows(weights, values):
    upper = weights.astype(jnp.bfloat16)
    lower = (weights - upper.astype(jnp.float32)).astype(jnp.bfloat16)
    first = jnp.dot(upper, values, preferred_element_type=jnp.float32)
    return first + jnp.dot(lower, values, preferred_element_type=jnp.float32)


def per_device(inputs, norm_gain, router, w_gate, w_up, w_down, routes):
    sections = lax.axis_size("section")
    section_at = lax.axis_index("section")
    owner_at = lax.axis_index("expert")
    slab_rows = inputs.shape[1]
    feature = inputs.shape[2]
    experts = router.shape[3]
    top_k = routes.shape[4]
    capacity = min(slab_rows, 3 * slab_rows * top_k // (2 * experts))
    step_count = 3 * sections - 1
    positions = lax.broadcasted_iota(jnp.int32, (1, 1, experts * capacity), 2)

    def layer(slab_in, moment):
        offset = moment - section_at
        is_busy = (offset >= 0) & (offset < 2 * sections)
        clipped = jnp.clip(offset, 0, 2 * sections - 1)
        loop_at = clipped // sections
        micro_at = clipped % sections
        gain_row = lax.dynamic_index_in_dim(norm_gain[:, 0], loop_at, 0, keepdims=False)
        router_now = lax.dynamic_index_in_dim(router[:, 0], loop_at, 0, keepdims=False)
        gate_mat = lax.dynamic_index_in_dim(w_gate[:, 0, 0], loop_at, 0, keepdims=False)
        up_mat = lax.dynamic_index_in_dim(w_up[:, 0, 0], loop_at, 0, keepdims=False)
        down_mat = lax.dynamic_index_in_dim(w_down[:, 0, 0], loop_at, 0, keepdims=False)
        routes_loop = lax.dynamic_index_in_dim(routes[:, 0], loop_at, 0, keepdims=False)
        routes_now = lax.dynamic_index_in_dim(routes_loop, micro_at, 0, keepdims=False)
        normed = normalize(slab_in, gain_row)
        own_routes = lax.dynamic_slice_in_dim(routes_now, owner_at * slab_rows, slab_rows, 0)
        gates = gate_weights(normed, router_now, own_routes)
        slots = slot_table(own_routes, slab_rows, experts)
        placed = own_routes * capacity + slots
        matches = placed[:, :, None] == positions
        select = jnp.any(matches, axis=1).astype(jnp.bfloat16)
        combine = jnp.sum(jnp.where(matches, gates[:, :, None], 0.0), axis=1)
        sending = jnp.einsum(
            "rp,rd->pd", select, normed, preferred_element_type=jnp.float32
        ).astype(jnp.bfloat16)
        sending = sending.reshape(experts, capacity, feature)
        received = lax.all_to_all(sending, "expert", split_axis=0, concat_axis=0, tiled=True)
        answered = lax.cond(
            is_busy,
            lambda values: expert_rows(values, gate_mat, up_mat, down_mat),
            jnp.zeros_like,
            received.reshape(-1, feature),
        ).reshape(received.shape)
        returned = lax.all_to_all(answered, "expert", split_axis=0, concat_axis=0, tiled=True)
        mixed = weighted_rows(combine, returned.reshape(-1, feature))
        return ((slab_in.astype(jnp.float32) + mixed).astype(jnp.bfloat16), micro_at)

    empty_slab = jnp.zeros_like(inputs[0])
    initial = (empty_slab, inputs[0], empty_slab)

    def advance(moment, loop_state):
        carried, feed_box, outbox = loop_state
        entering = (section_at == 0) & (moment < sections)
        fresh = feed_box
        slab_in = jnp.where(entering, fresh, carried)
        result, micro_at = layer(slab_in, moment)
        carried = passed_along(result, "section", 1)
        finish = (section_at == sections - 1) & (moment >= 2 * sections - 1)
        feed_box, outbox = passed_along_2((feed_box, outbox), "section", -1)
        outbox = jnp.where(finish, result, outbox)
        return (carried, feed_box, outbox)

    loop_state = lax.fori_loop(0, step_count, advance, initial)
    return loop_state[2][None]


def solution(mesh):
    return jax.shard_map(
        per_device,
        mesh=mesh,
        in_specs=(
            P("section", "expert", None),
            P(None, "section", None),
            P(None, "section", None, None),
            P(None, "section", "expert", None, None),
            P(None, "section", "expert", None, None),
            P(None, "section", "expert", None, None),
            P(None, "section", None, None, None),
        ),
        out_specs=P("section", "expert", None),
        check_vma=False,
    )
```

profile of v0, /device:TPU:20, one launch (start us, length us, event | category | flops | bytes accessed | tf_op | source)
XLA Modules:
  0.0 453.2 jit_solution(15295944289878618531)
XLA Ops:
  0.9 451.7 %while.21 = (s32[]{:T(128)}, bf16[16,2560]{1,0:T(8,128)(2,1)S(1)}, bf16[16,2560]{1,0:T(8,128)(2,1)S(1)}, bf16[16,2560]{1,0:T(8,128)(2,1)S(1)}, pred[]{:T(512)}, ...) while((s32[]{:T(128)}, bf16[16,2560]{1,0:T(8,128)(2,1)S(1)}, ...), condition=%wide.region_10.11_spmd.clone, body=%wide.region_0.10_spmd.clone.sunk | while | flops 1737769472 | bytes 32948616 | solution.py:119
  5.3 6.2 %all-to-all-start = ((bf16[16,9,2560]{2,1,0:T(8,128)(2,1)}), bf16[16,9,2560]{2,1,0:T(8,128)(2,1)S(1)}, u32[]{:S(2)}, u32[]{:S(2)}) async-start(bf16[16,9,2560]{2,1,0:T(8,128)(2,1)} %reshape.244), calls=%async_computation | async-start | bytes 2621440 | tf_op jit(solution)/shard_map/while/body/eval_jaxpr/all_to_all | solution.py:93
  13.8 28.4 %all-to-all-done = bf16[16,9,2560]{2,1,0:T(8,128)(2,1)S(1)} async-done(((bf16[16,9,2560]{2,1,0:T(8,128)(2,1)}), bf16[16,9,2560]{2,1,0:T(8,128)(2,1)S(1)}, u32[]{:S(2)}, u32[]{:S(2)}) %all-to-all-start) | async-done | bytes 737312 | tf_op jit(solution)/shard_map/while/body/eval_jaxpr/all_to_all | solution.py:93
  48.3 10.6 %collective-permute-start = (bf16[16,2560]{1,0:T(8,128)(2,1)S(1)}, bf16[16,2560]{1,0:T(8,128)(2,1)S(1)}, u32[]{:S(2)}, u32[]{:S(2)}) collective-permute-start(bf16[16,2560]{1,0:T(8,128)(2,1)S(1)} %broadcast_select_fusion.6), channel_id=1, source_target_pairs={{16,0},{17,1},{18,2},{19,3},{20,4},{21,5},{22,6},{23,7},{24,8},{25... | collective-permute-start | bytes 245768 | tf_op jit(solution)/shard_map/while/body/eval_jaxpr/ppermute | solution.py:15
  59.5 19.6 %all-to-all-done.1 = bf16[16,9,2560]{2,1,0:T(8,128)(2,1)S(1)} async-done(((bf16[16,9,2560]{2,1,0:T(8,128)(2,1)}), bf16[16,9,2560]{2,1,0:T(8,128)(2,1)S(1)}, u32[]{:S(2)}, u32[]{:S(2)}) %all-to-all-start.1) | async-done | bytes 737312 | tf_op jit(solution)/shard_map/while/body/eval_jaxpr/all_to_all | solution.py:100
  79.8 8.8 %collective-permute-start.1 = (bf16[16,2560]{1,0:T(8,128)(2,1)S(1)}, bf16[16,2560]{1,0:T(8,128)(2,1)S(1)}, u32[]{:S(2)}, u32[]{:S(2)}) collective-permute-start(bf16[16,2560]{1,0:T(8,128)(2,1)S(1)} %get-tuple-element.674), channel_id=1, source_target_pairs={{0,16},{16,0},{1,17},{17,1},{2,18},{18,2},{3,19},{19,3},{4,20},{20... | collective-permute-start | bytes 245768 | tf_op jit(solution)/shard_map/while/body/eval_jaxpr/ppermute | solution.py:9
  95.4 5.1 %all-to-all-start = ((bf16[16,9,2560]{2,1,0:T(8,128)(2,1)}), bf16[16,9,2560]{2,1,0:T(8,128)(2,1)S(1)}, u32[]{:S(2)}, u32[]{:S(2)}) async-start(bf16[16,9,2560]{2,1,0:T(8,128)(2,1)} %reshape.244), calls=%async_computation | async-start | bytes 2621440 | tf_op jit(solution)/shard_map/while/body/eval_jaxpr/all_to_all | solution.py:93
  104.2 27.1 %all-to-all-done = bf16[16,9,2560]{2,1,0:T(8,128)(2,1)S(1)} async-done(((bf16[16,9,2560]{2,1,0:T(8,128)(2,1)}), bf16[16,9,2560]{2,1,0:T(8,128)(2,1)S(1)}, u32[]{:S(2)}, u32[]{:S(2)}) %all-to-all-start) | async-done | bytes 737312 | tf_op jit(solution)/shard_map/while/body/eval_jaxpr/all_to_all | solution.py:93
  131.3 8.3 %conditional.3 = (bf16[144,2560]{1,0:T(8,128)(2,1)S(1)}) conditional(s32[]{:T(128)} %convert_element_type.207, () %tuple.69, (bf16[2,1,1,2560,768]{4,3,2,1,0:T(8,128)(2,1)}, s32[]{:T(128)}, bf16[16,9,2560]{2,1,0:T(8,128)(2,1)S(1)}, bf16[2,1,1,2560,768]{4,3,2,1,0:T(8,128)(2,1)}, bf16[2,1,1,768,2560]{4,3,2,1,0:T(8,128)(2,1)}) %tuple.70), branch_computations={%region_8.8_spmd, %region_9.9_spmd} | conditional | flops 1699725312 | bytes 16369160 | solution.py:94
  134.5 5.1 %fusion.11 = bf16[144,2560]{1,0:T(8,128)(2,1)S(1)} fusion(bf16[2,1,1,768,2560]{4,3,2,1,0:T(8,128)(2,1)} %get-tuple-element.443, s32[]{:T(128)} %get-tuple-element.440, bf16[144,2560]{1,0:T(8,128)(2,1)S(1)} %reshape.229, bf16[2,1,1,2560,768]{4,3,2,1,0:T(8,128)(2,1)} %get-tuple-element.442, f32[144,768]{1,0:T(8,128)S(1)} %fusion.14), kind=kOutput, calls=%fused_computation.10 | convolution fusion | flops 1133494272 | bytes 9782272 | tf_op jit(solution)/shard_map/while/body/eval_jaxpr/cond/branch_1_fun/dot_general | solution.py:46
  149.8 26.5 %all-to-all-done.1 = bf16[16,9,2560]{2,1,0:T(8,128)(2,1)S(1)} async-done(((bf16[16,9,2560]{2,1,0:T(8,128)(2,1)}), bf16[16,9,2560]{2,1,0:T(8,128)(2,1)S(1)}, u32[]{:S(2)}, u32[]{:S(2)}) %all-to-all-start.1) | async-done | bytes 737312 | tf_op jit(solution)/shard_map/while/body/eval_jaxpr/all_to_all | solution.py:100
  194.5 27.1 %all-to-all-done = bf16[16,9,2560]{2,1,0:T(8,128)(2,1)S(1)} async-done(((bf16[16,9,2560]{2,1,0:T(8,128)(2,1)}), bf16[16,9,2560]{2,1,0:T(8,128)(2,1)S(1)}, u32[]{:S(2)}, u32[]{:S(2)}) %all-to-all-start) | async-done | bytes 737312 | tf_op jit(solution)/shard_map/while/body/eval_jaxpr/all_to_all | solution.py:93
  221.6 8.3 %conditional.3 = (bf16[144,2560]{1,0:T(8,128)(2,1)S(1)}) conditional(s32[]{:T(128)} %convert_element_type.207, () %tuple.69, (bf16[2,1,1,2560,768]{4,3,2,1,0:T(8,128)(2,1)}, s32[]{:T(128)}, bf16[16,9,2560]{2,1,0:T(8,128)(2,1)S(1)}, bf16[2,1,1,2560,768]{4,3,2,1,0:T(8,128)(2,1)}, bf16[2,1,1,768,2560]{4,3,2,1,0:T(8,128)(2,1)}) %tuple.70), branch_computations={%region_8.8_spmd, %region_9.9_spmd} | conditional | flops 1699725312 | bytes 16369160 | solution.py:94
  224.8 5.1 %fusion.11 = bf16[144,2560]{1,0:T(8,128)(2,1)S(1)} fusion(bf16[2,1,1,768,2560]{4,3,2,1,0:T(8,128)(2,1)} %get-tuple-element.443, s32[]{:T(128)} %get-tuple-element.440, bf16[144,2560]{1,0:T(8,128)(2,1)S(1)} %reshape.229, bf16[2,1,1,2560,768]{4,3,2,1,0:T(8,128)(2,1)} %get-tuple-element.442, f32[144,768]{1,0:T(8,128)S(1)} %fusion.14), kind=kOutput, calls=%fused_computation.10 | convolution fusion | flops 1133494272 | bytes 9782272 | tf_op jit(solution)/shard_map/while/body/eval_jaxpr/cond/branch_1_fun/dot_general | solution.py:46
  240.1 26.5 %all-to-all-done.1 = bf16[16,9,2560]{2,1,0:T(8,128)(2,1)S(1)} async-done(((bf16[16,9,2560]{2,1,0:T(8,128)(2,1)}), bf16[16,9,2560]{2,1,0:T(8,128)(2,1)S(1)}, u32[]{:S(2)}, u32[]{:S(2)}) %all-to-all-start.1) | async-done | bytes 737312 | tf_op jit(solution)/shard_map/while/body/eval_jaxpr/all_to_all | solution.py:100
  276.3 4.8 %all-to-all-start = ((bf16[16,9,2560]{2,1,0:T(8,128)(2,1)}), bf16[16,9,2560]{2,1,0:T(8,128)(2,1)S(1)}, u32[]{:S(2)}, u32[]{:S(2)}) async-start(bf16[16,9,2560]{2,1,0:T(8,128)(2,1)} %reshape.244), calls=%async_computation | async-start | bytes 2621440 | tf_op jit(solution)/shard_map/while/body/eval_jaxpr/all_to_all | solution.py:93
  284.8 27.1 %all-to-all-done = bf16[16,9,2560]{2,1,0:T(8,128)(2,1)S(1)} async-done(((bf16[16,9,2560]{2,1,0:T(8,128)(2,1)}), bf16[16,9,2560]{2,1,0:T(8,128)(2,1)S(1)}, u32[]{:S(2)}, u32[]{:S(2)}) %all-to-all-start) | async-done | bytes 737312 | tf_op jit(solution)/shard_map/while/body/eval_jaxpr/all_to_all | solution.py:93
  311.9 8.3 %conditional.3 = (bf16[144,2560]{1,0:T(8,128)(2,1)S(1)}) conditional(s32[]{:T(128)} %convert_element_type.207, () %tuple.69, (bf16[2,1,1,2560,768]{4,3,2,1,0:T(8,128)(2,1)}, s32[]{:T(128)}, bf16[16,9,2560]{2,1,0:T(8,128)(2,1)S(1)}, bf16[2,1,1,2560,768]{4,3,2,1,0:T(8,128)(2,1)}, bf16[2,1,1,768,2560]{4,3,2,1,0:T(8,128)(2,1)}) %tuple.70), branch_computations={%region_8.8_spmd, %region_9.9_spmd} | conditional | flops 1699725312 | bytes 16369160 | solution.py:94
  315.1 5.1 %fusion.11 = bf16[144,2560]{1,0:T(8,128)(2,1)S(1)} fusion(bf16[2,1,1,768,2560]{4,3,2,1,0:T(8,128)(2,1)} %get-tuple-element.443, s32[]{:T(128)} %get-tuple-element.440, bf16[144,2560]{1,0:T(8,128)(2,1)S(1)} %reshape.229, bf16[2,1,1,2560,768]{4,3,2,1,0:T(8,128)(2,1)} %get-tuple-element.442, f32[144,768]{1,0:T(8,128)S(1)} %fusion.14), kind=kOutput, calls=%fused_computation.10 | convolution fusion | flops 1133494272 | bytes 9782272 | tf_op jit(solution)/shard_map/while/body/eval_jaxpr/cond/branch_1_fun/dot_general | solution.py:46
  330.5 26.5 %all-to-all-done.1 = bf16[16,9,2560]{2,1,0:T(8,128)(2,1)S(1)} async-done(((bf16[16,9,2560]{2,1,0:T(8,128)(2,1)}), bf16[16,9,2560]{2,1,0:T(8,128)(2,1)S(1)}, u32[]{:S(2)}, u32[]{:S(2)}) %all-to-all-start.1) | async-done | bytes 737312 | tf_op jit(solution)/shard_map/while/body/eval_jaxpr/all_to_all | solution.py:100
  375.1 27.1 %all-to-all-done = bf16[16,9,2560]{2,1,0:T(8,128)(2,1)S(1)} async-done(((bf16[16,9,2560]{2,1,0:T(8,128)(2,1)}), bf16[16,9,2560]{2,1,0:T(8,128)(2,1)S(1)}, u32[]{:S(2)}, u32[]{:S(2)}) %all-to-all-start) | async-done | bytes 737312 | tf_op jit(solution)/shard_map/while/body/eval_jaxpr/all_to_all | solution.py:93
  402.2 8.3 %conditional.3 = (bf16[144,2560]{1,0:T(8,128)(2,1)S(1)}) conditional(s32[]{:T(128)} %convert_element_type.207, () %tuple.69, (bf16[2,1,1,2560,768]{4,3,2,1,0:T(8,128)(2,1)}, s32[]{:T(128)}, bf16[16,9,2560]{2,1,0:T(8,128)(2,1)S(1)}, bf16[2,1,1,2560,768]{4,3,2,1,0:T(8,128)(2,1)}, bf16[2,1,1,768,2560]{4,3,2,1,0:T(8,128)(2,1)}) %tuple.70), branch_computations={%region_8.8_spmd, %region_9.9_spmd} | conditional | flops 1699725312 | bytes 16369160 | solution.py:94
  405.4 5.1 %fusion.11 = bf16[144,2560]{1,0:T(8,128)(2,1)S(1)} fusion(bf16[2,1,1,768,2560]{4,3,2,1,0:T(8,128)(2,1)} %get-tuple-element.443, s32[]{:T(128)} %get-tuple-element.440, bf16[144,2560]{1,0:T(8,128)(2,1)S(1)} %reshape.229, bf16[2,1,1,2560,768]{4,3,2,1,0:T(8,128)(2,1)} %get-tuple-element.442, f32[144,768]{1,0:T(8,128)S(1)} %fusion.14), kind=kOutput, calls=%fused_computation.10 | convolution fusion | flops 1133494272 | bytes 9782272 | tf_op jit(solution)/shard_map/while/body/eval_jaxpr/cond/branch_1_fun/dot_general | solution.py:46
  418.4 28.9 %all-to-all-done.1 = bf16[16,9,2560]{2,1,0:T(8,128)(2,1)S(1)} async-done(((bf16[16,9,2560]{2,1,0:T(8,128)(2,1)}), bf16[16,9,2560]{2,1,0:T(8,128)(2,1)S(1)}, u32[]{:S(2)}, u32[]{:S(2)}) %all-to-all-start.1) | async-done | bytes 737312 | tf_op jit(solution)/shard_map/while/body/eval_jaxpr/all_to_all | solution.py:100
  (195 shorter events, 131.4 us)
Async XLA Ops:
  5.3 37.0 %all-to-all-start = ((bf16[16,9,2560]{2,1,0:T(8,128)(2,1)}), bf16[16,9,2560]{2,1,0:T(8,128)(2,1)S(1)}, u32[]{:S(2)}, u32[]{:S(2)}) async-start(bf16[16,9,2560]{2,1,0:T(8,128)(2,1)} %reshape.244), calls=%async_computation | async-start | bytes 2621440 | tf_op jit(solution)/shard_map/while/body/eval_jaxpr/all_to_all | solution.py:93
  11.4 77.2 %collective-permute-start.2 = (bf16[16,2560]{1,0:T(8,128)(2,1)S(1)}, bf16[16,2560]{1,0:T(8,128)(2,1)S(1)}, u32[]{:S(2)}, u32[]{:S(2)}) collective-permute-start(bf16[16,2560]{1,0:T(8,128)(2,1)S(1)} %copy.43), channel_id=1, source_target_pairs={{16,0},{17,1},{18,2},{19,3},{20,4},{21,5},{22,6},{23,7},{24,8},{25... | collective-permute-start | bytes 245768 | tf_op jit(solution)/shard_map/while/body/eval_jaxpr/ppermute | solution.py:15
  43.7 35.4 %all-to-all-start.1 = ((bf16[16,9,2560]{2,1,0:T(8,128)(2,1)}), bf16[16,9,2560]{2,1,0:T(8,128)(2,1)S(1)}, u32[]{:S(2)}, u32[]{:S(2)}) async-start(bf16[16,9,2560]{2,1,0:T(8,128)(2,1)} %reshape.245), calls=%async_computation.1 | async-start | bytes 2621440 | tf_op jit(solution)/shard_map/while/body/eval_jaxpr/all_to_all | solution.py:100
  48.3 31.3 %collective-permute-start = (bf16[16,2560]{1,0:T(8,128)(2,1)S(1)}, bf16[16,2560]{1,0:T(8,128)(2,1)S(1)}, u32[]{:S(2)}, u32[]{:S(2)}) collective-permute-start(bf16[16,2560]{1,0:T(8,128)(2,1)S(1)} %broadcast_select_fusion.6), channel_id=1, source_target_pairs={{16,0},{17,1},{18,2},{19,3},{20,4},{21,5},{22,6},{23,7},{24,8},{25... | collective-permute-start | bytes 245768 | tf_op jit(solution)/shard_map/while/body/eval_jaxpr/ppermute | solution.py:15
  79.8 11.2 %collective-permute-start.1 = (bf16[16,2560]{1,0:T(8,128)(2,1)S(1)}, bf16[16,2560]{1,0:T(8,128)(2,1)S(1)}, u32[]{:S(2)}, u32[]{:S(2)}) collective-permute-start(bf16[16,2560]{1,0:T(8,128)(2,1)S(1)} %get-tuple-element.674), channel_id=1, source_target_pairs={{0,16},{16,0},{1,17},{17,1},{2,18},{18,2},{3,19},{19,3},{4,20},{20... | collective-permute-start | bytes 245768 | tf_op jit(solution)/shard_map/while/body/eval_jaxpr/ppermute | solution.py:9
  95.4 35.9 %all-to-all-start = ((bf16[16,9,2560]{2,1,0:T(8,128)(2,1)}), bf16[16,9,2560]{2,1,0:T(8,128)(2,1)S(1)}, u32[]{:S(2)}, u32[]{:S(2)}) async-start(bf16[16,9,2560]{2,1,0:T(8,128)(2,1)} %reshape.244), calls=%async_computation | async-start | bytes 2621440 | tf_op jit(solution)/shard_map/while/body/eval_jaxpr/all_to_all | solution.py:93
  100.5 78.5 %collective-permute-start.2 = (bf16[16,2560]{1,0:T(8,128)(2,1)S(1)}, bf16[16,2560]{1,0:T(8,128)(2,1)S(1)}, u32[]{:S(2)}, u32[]{:S(2)}) collective-permute-start(bf16[16,2560]{1,0:T(8,128)(2,1)S(1)} %copy.43), channel_id=1, source_target_pairs={{16,0},{17,1},{18,2},{19,3},{20,4},{21,5},{22,6},{23,7},{24,8},{25... | collective-permute-start | bytes 245768 | tf_op jit(solution)/shard_map/while/body/eval_jaxpr/ppermute | solution.py:15
  140.9 35.4 %all-to-all-start.1 = ((bf16[16,9,2560]{2,1,0:T(8,128)(2,1)}), bf16[16,9,2560]{2,1,0:T(8,128)(2,1)S(1)}, u32[]{:S(2)}, u32[]{:S(2)}) async-start(bf16[16,9,2560]{2,1,0:T(8,128)(2,1)} %reshape.245), calls=%async_computation.1 | async-start | bytes 2621440 | tf_op jit(solution)/shard_map/while/body/eval_jaxpr/all_to_all | solution.py:100
  145.6 31.3 %collective-permute-start = (bf16[16,2560]{1,0:T(8,128)(2,1)S(1)}, bf16[16,2560]{1,0:T(8,128)(2,1)S(1)}, u32[]{:S(2)}, u32[]{:S(2)}) collective-permute-start(bf16[16,2560]{1,0:T(8,128)(2,1)S(1)} %broadcast_select_fusion.6), channel_id=1, source_target_pairs={{16,0},{17,1},{18,2},{19,3},{20,4},{21,5},{22,6},{23,7},{24,8},{25... | collective-permute-start | bytes 245768 | tf_op jit(solution)/shard_map/while/body/eval_jaxpr/ppermute | solution.py:15
  177.1 4.5 collective-permute-start.1
  186.0 35.6 %all-to-all-start = ((bf16[16,9,2560]{2,1,0:T(8,128)(2,1)}), bf16[16,9,2560]{2,1,0:T(8,128)(2,1)S(1)}, u32[]{:S(2)}, u32[]{:S(2)}) async-start(bf16[16,9,2560]{2,1,0:T(8,128)(2,1)} %reshape.244), calls=%async_computation | async-start | bytes 2621440 | tf_op jit(solution)/shard_map/while/body/eval_jaxpr/all_to_all | solution.py:93
  190.8 78.5 %collective-permute-start.2 = (bf16[16,2560]{1,0:T(8,128)(2,1)S(1)}, bf16[16,2560]{1,0:T(8,128)(2,1)S(1)}, u32[]{:S(2)}, u32[]{:S(2)}) collective-permute-start(bf16[16,2560]{1,0:T(8,128)(2,1)S(1)} %copy.43), channel_id=1, source_target_pairs={{16,0},{17,1},{18,2},{19,3},{20,4},{21,5},{22,6},{23,7},{24,8},{25... | collective-permute-start | bytes 245768 | tf_op jit(solution)/shard_map/while/body/eval_jaxpr/ppermute | solution.py:15
  231.3 35.4 %all-to-all-start.1 = ((bf16[16,9,2560]{2,1,0:T(8,128)(2,1)}), bf16[16,9,2560]{2,1,0:T(8,128)(2,1)S(1)}, u32[]{:S(2)}, u32[]{:S(2)}) async-start(bf16[16,9,2560]{2,1,0:T(8,128)(2,1)} %reshape.245), calls=%async_computation.1 | async-start | bytes 2621440 | tf_op jit(solution)/shard_map/while/body/eval_jaxpr/all_to_all | solution.py:100
  235.9 31.3 %collective-permute-start = (bf16[16,2560]{1,0:T(8,128)(2,1)S(1)}, bf16[16,2560]{1,0:T(8,128)(2,1)S(1)}, u32[]{:S(2)}, u32[]{:S(2)}) collective-permute-start(bf16[16,2560]{1,0:T(8,128)(2,1)S(1)} %broadcast_select_fusion.6), channel_id=1, source_target_pairs={{16,0},{17,1},{18,2},{19,3},{20,4},{21,5},{22,6},{23,7},{24,8},{25... | collective-permute-start | bytes 245768 | tf_op jit(solution)/shard_map/while/body/eval_jaxpr/ppermute | solution.py:15
  276.3 35.6 %all-to-all-start = ((bf16[16,9,2560]{2,1,0:T(8,128)(2,1)}), bf16[16,9,2560]{2,1,0:T(8,128)(2,1)S(1)}, u32[]{:S(2)}, u32[]{:S(2)}) async-start(bf16[16,9,2560]{2,1,0:T(8,128)(2,1)} %reshape.244), calls=%async_computation | async-start | bytes 2621440 | tf_op jit(solution)/shard_map/while/body/eval_jaxpr/all_to_all | solution.py:93
  281.1 78.5 %collective-permute-start.2 = (bf16[16,2560]{1,0:T(8,128)(2,1)S(1)}, bf16[16,2560]{1,0:T(8,128)(2,1)S(1)}, u32[]{:S(2)}, u32[]{:S(2)}) collective-permute-start(bf16[16,2560]{1,0:T(8,128)(2,1)S(1)} %copy.43), channel_id=1, source_target_pairs={{16,0},{17,1},{18,2},{19,3},{20,4},{21,5},{22,6},{23,7},{24,8},{25... | collective-permute-start | bytes 245768 | tf_op jit(solution)/shard_map/while/body/eval_jaxpr/ppermute | solution.py:15
  321.6 35.4 %all-to-all-start.1 = ((bf16[16,9,2560]{2,1,0:T(8,128)(2,1)}), bf16[16,9,2560]{2,1,0:T(8,128)(2,1)S(1)}, u32[]{:S(2)}, u32[]{:S(2)}) async-start(bf16[16,9,2560]{2,1,0:T(8,128)(2,1)} %reshape.245), calls=%async_computation.1 | async-start | bytes 2621440 | tf_op jit(solution)/shard_map/while/body/eval_jaxpr/all_to_all | solution.py:100
  326.2 31.3 %collective-permute-start = (bf16[16,2560]{1,0:T(8,128)(2,1)S(1)}, bf16[16,2560]{1,0:T(8,128)(2,1)S(1)}, u32[]{:S(2)}, u32[]{:S(2)}) collective-permute-start(bf16[16,2560]{1,0:T(8,128)(2,1)S(1)} %broadcast_select_fusion.6), channel_id=1, source_target_pairs={{16,0},{17,1},{18,2},{19,3},{20,4},{21,5},{22,6},{23,7},{24,8},{25... | collective-permute-start | bytes 245768 | tf_op jit(solution)/shard_map/while/body/eval_jaxpr/ppermute | solution.py:15
  357.7 4.5 collective-permute-start.1
  366.6 35.6 %all-to-all-start = ((bf16[16,9,2560]{2,1,0:T(8,128)(2,1)}), bf16[16,9,2560]{2,1,0:T(8,128)(2,1)S(1)}, u32[]{:S(2)}, u32[]{:S(2)}) async-start(bf16[16,9,2560]{2,1,0:T(8,128)(2,1)} %reshape.244), calls=%async_computation | async-start | bytes 2621440 | tf_op jit(solution)/shard_map/while/body/eval_jaxpr/all_to_all | solution.py:93
  371.4 76.7 %collective-permute-start.2 = (bf16[16,2560]{1,0:T(8,128)(2,1)S(1)}, bf16[16,2560]{1,0:T(8,128)(2,1)S(1)}, u32[]{:S(2)}, u32[]{:S(2)}) collective-permute-start(bf16[16,2560]{1,0:T(8,128)(2,1)S(1)} %copy.43), channel_id=1, source_target_pairs={{16,0},{17,1},{18,2},{19,3},{20,4},{21,5},{22,6},{23,7},{24,8},{25... | collective-permute-start | bytes 245768 | tf_op jit(solution)/shard_map/while/body/eval_jaxpr/ppermute | solution.py:15
  411.9 35.4 %all-to-all-start.1 = ((bf16[16,9,2560]{2,1,0:T(8,128)(2,1)}), bf16[16,9,2560]{2,1,0:T(8,128)(2,1)S(1)}, u32[]{:S(2)}, u32[]{:S(2)}) async-start(bf16[16,9,2560]{2,1,0:T(8,128)(2,1)} %reshape.245), calls=%async_computation.1 | async-start | bytes 2621440 | tf_op jit(solution)/shard_map/while/body/eval_jaxpr/all_to_all | solution.py:100
  416.5 31.3 %collective-permute-start = (bf16[16,2560]{1,0:T(8,128)(2,1)S(1)}, bf16[16,2560]{1,0:T(8,128)(2,1)S(1)}, u32[]{:S(2)}, u32[]{:S(2)}) collective-permute-start(bf16[16,2560]{1,0:T(8,128)(2,1)S(1)} %broadcast_select_fusion.6), channel_id=1, source_target_pairs={{16,0},{17,1},{18,2},{19,3},{20,4},{21,5},{22,6},{23,7},{24,8},{25... | collective-permute-start | bytes 245768 | tf_op jit(solution)/shard_map/while/body/eval_jaxpr/ppermute | solution.py:15
  448.1 4.5 collective-permute-start.1
  (7 other events, 58.3 us)
where the time goes:
time: 455 us; the launch traced here: 453 us
  waiting for transfers between devices  280 us (62%)
  starting transfers between devices  103 us (23%)
  matrix products  37 us (8%)
  local copies, waits for them, and re-layouts  27.4 us (6%)
  other arithmetic  4.87 us (1%)
    all_to_all x5, waiting for transfers between devices, layer(): lax.all_to_all(sending, 'expert', split_axis=0, concat_axis=0, tiled=True)  137 us
    all_to_all x5, waiting for transfers between devices, layer(): lax.all_to_all(answered, 'expert', split_axis=0, concat_axis=0, tiled=True)  128 us
    ppermute x10, starting transfers between devices, passed_along_2(): return lax.ppermute(block, axis, route)  39.8 us
    all_to_all x5, starting transfers between devices, layer(): lax.all_to_all(sending, 'expert', split_axis=0, concat_axis=0, tiled=True)  25.8 us
    all_to_all x5, starting transfers between devices, layer(): lax.all_to_all(answered, 'expert', split_axis=0, concat_axis=0, tiled=True)  23.2 us
    dot_general x4, matrix products, expert_rows(): jnp.dot(hidden, down_mat, preferred_element_type=jnp.float32)  20.4 us
    ppermute x5, waiting for transfers between devices, passed_along(): lax.ppermute(array, axis, [(i, (i + by) % size) for i in range(size)])  14.9 us
    ppermute x5, starting transfers between devices, passed_along(): lax.ppermute(array, axis, [(i, (i + by) % size) for i in range(size)])  14.3 us
  transfers between devices with their start and end apart: 25, of which 15 were waited for; matrix products, arithmetic and copies ran while one was open for 10% of the time, Pallas kernels for 0%

commit v1 on v0

--- a/solution.py
+++ b/solution.py
@@ -2,6 +2,36 @@
 import jax.numpy as jnp
 from jax import lax
 from jax.sharding import PartitionSpec as P
+
+
+def switch_weights_on(own_rows, d_out, xs):
+    taken_in = own_rows.shape
+    return jnp.moveaxis(
+        own_rows.reshape(*taken_in[:d_out], xs, taken_in[d_out] // xs, *taken_in[d_out + 1 :]),
+        d_out,
+        0,
+    )
+
+
+def convert_sheet(row_data, along_dim):
+    row_data = jnp.moveaxis(row_data, 0, along_dim)
+    passed = row_data.shape
+    return row_data.reshape(
+        *passed[:along_dim], passed[along_dim] * passed[along_dim + 1], *passed[along_dim + 2 :]
+    )
+
+
+def table_load(t0, bus_axis, vec, my_tile):
+    current_block, y1 = (lax.axis_size(bus_axis), lax.axis_index(bus_axis))
+    t_next = switch_weights_on(t0, vec, current_block)
+    row_list = [t_next[y1]]
+    for p in range(1, current_block):
+        s_next = t_next[y1 ^ p]
+        row_list.append(
+            lax.ppermute(s_next, bus_axis, [(dev_i, dev_i ^ p) for dev_i in range(current_block)])
+        )
+    t_next = jnp.stack(row_list, axis=0)[y1 ^ jnp.arange(current_block)]
+    return convert_sheet(t_next, my_tile)
 
 
 def passed_along(array, axis, by):
@@ -97,7 +127,7 @@
             jnp.zeros_like,
             received.reshape(-1, feature),
         ).reshape(received.shape)
-        returned = lax.all_to_all(answered, "expert", split_axis=0, concat_axis=0, tiled=True)
+        returned = table_load(answered, "expert", 0, 0)
         mixed = weighted_rows(combine, returned.reshape(-1, feature))
         return ((slab_in.astype(jnp.float32) + mixed).astype(jnp.bfloat16), micro_at)
 

time: 455 us -> 506 us (1.11)
  starting transfers between devices: 103 us -> 135 us
  local copies, waits for them, and re-layouts: 27.4 us -> 35 us
    all_to_all x5 -> x0, waiting for transfers between devices: 128 us -> none  [layer(): lax.all_to_all(answered, 'expert', split_axis=0, concat_axis=0, tiled=True)]
    ppermute x0 -> x75, waiting for transfers between devices: none -> 126 us  [table_load(): lax.ppermute(s_next, bus_axis, [(dev_i, dev_i ^ p) for dev_i in range(cur...]
    ppermute x0 -> x75, starting transfers between devices: none -> 75.8 us  [table_load(): lax.ppermute(s_next, bus_axis, [(dev_i, dev_i ^ p) for dev_i in range(cur...]
    all_to_all x5 -> x0, starting transfers between devices: 23.2 us -> none  [layer(): lax.all_to_all(answered, 'expert', split_axis=0, concat_axis=0, tiled=True)]
    ppermute x10, starting transfers between devices: 39.8 us -> 25.3 us  [passed_along_2(): return lax.ppermute(block, axis, route)]
    ppermute x5, starting transfers between devices: 14.3 us -> 7.62 us  [passed_along(): lax.ppermute(array, axis, [(i, (i + by) % size) for i in range(size)])]
    ppermute x5, waiting for transfers between devices: 14.9 us -> 20.5 us  [passed_along(): lax.ppermute(array, axis, [(i, (i + by) % size) for i in range(size)])]
    reshape x5, local copies, waits for them, and re-layouts: 6.79 us -> 1.3 us  [switch_weights_on(): own_rows.reshape(*taken_in[:d_out], xs, taken_in[d_out] // xs, *taken_in[...]
  transfers between devices with their start and end apart: 25 -> 95, of which waited for: 15 -> 70; matrix products, arithmetic and copies ran while one was open for 10% -> 15% of each run, Pallas kernels for 0% -> 0%
where the time goes in v1:
time: 506 us; the launch traced here: 504 us
  waiting for transfers between devices  285 us (56%)
  starting transfers between devices  135 us (27%)
  matrix products  39.7 us (8%)
  local copies, waits for them, and re-layouts  35 us (7%)
  other arithmetic  8.13 us (2%)
    all_to_all x5, waiting for transfers between devices, layer(): lax.all_to_all(sending, 'expert', split_axis=0, concat_axis=0, tiled=True)  138 us
    ppermute x75, waiting for transfers between devices, table_load(): lax.ppermute(s_next, bus_axis, [(dev_i, dev_i ^ p) for dev_i in range(cur...  126 us
    ppermute x75, starting transfers between devices, table_load(): lax.ppermute(s_next, bus_axis, [(dev_i, dev_i ^ p) for dev_i in range(cur...  75.8 us
    all_to_all x5, starting transfers between devices, layer(): lax.all_to_all(sending, 'expert', split_axis=0, concat_axis=0, tiled=True)  26.3 us
    ppermute x10, starting transfers between devices, passed_along_2(): return lax.ppermute(block, axis, route)  25.3 us
    ppermute x5, waiting for transfers between devices, passed_along(): lax.ppermute(array, axis, [(i, (i + by) % size) for i in range(size)])  20.5 us
    dot_general x4, matrix products, expert_rows(): jnp.dot(hidden, down_mat, preferred_element_type=jnp.float32)  20.4 us
    dot_general x4, matrix products, expert_rows(): gate_proj = jnp.dot(rows_in, gate_mat, preferred_element_type=jnp.float32)  11.4 us
  transfers between devices with their start and end apart: 95, of which 70 were waited for; matrix products, arithmetic and copies ran while one was open for 15% of the time, Pallas kernels for 0%

profile of v1, /device:TPU:20, one launch (start us, length us, event | category | flops | bytes accessed | tf_op | source)
XLA Modules:
  0.0 503.7 jit_solution(9480127422657687404)
XLA Ops:
  1.5 501.5 %while.21 = (s32[]{:T(128)}, bf16[16,2560]{1,0:T(8,128)(2,1)S(1)}, bf16[16,2560]{1,0:T(8,128)(2,1)}, bf16[16,2560]{1,0:T(8,128)(2,1)S(1)}, pred[]{:T(512)}, /*in...) while((s32[]{:T(128)}, bf16[16,2560]{1,0:T(8,128)(2,1)S(1)}, ...), condition=%wide.region_10.11_spmd.clone, body=%wide.region_0.10_spmd.clone.sunk | while | flops 1737770624 | bytes 38125556 | solution.py:149
  9.8 6.3 %all-to-all-start = ((bf16[16,9,2560]{2,1,0:T(8,128)(2,1)}), bf16[16,9,2560]{2,1,0:T(8,128)(2,1)S(1)}, u32[]{:S(2)}, u32[]{:S(2)}) async-start(bf16[16,9,2560]{2,1,0:T(8,128)(2,1)} %reshape.280), calls=%async_computation | async-start | bytes 2621440 | tf_op jit(solution)/shard_map/while/body/eval_jaxpr/all_to_all | solution.py:123
  19.2 27.7 %all-to-all-done = bf16[16,9,2560]{2,1,0:T(8,128)(2,1)S(1)} async-done(((bf16[16,9,2560]{2,1,0:T(8,128)(2,1)}), bf16[16,9,2560]{2,1,0:T(8,128)(2,1)S(1)}, u32[]{:S(2)}, u32[]{:S(2)}) %all-to-all-start) | async-done | bytes 737312 | tf_op jit(solution)/shard_map/while/body/eval_jaxpr/all_to_all | solution.py:123
  90.7 7.3 %collective-permute-start.16 = (bf16[16,2560]{1,0:T(8,128)(2,1)S(1)}, bf16[16,2560]{1,0:T(8,128)(2,1)S(1)}, u32[]{:S(2)}, u32[]{:S(2)}) collective-permute-start(bf16[16,2560]{1,0:T(8,128)(2,1)S(1)} %get-tuple-element.723), channel_id=1, source_target_pairs={{0,16},{16,0},{1,17},{17,1},{2,18},{18,2},{3,19},{19,3},{4,20},{20... | collective-permute-start | bytes 245768 | tf_op jit(solution)/shard_map/while/body/eval_jaxpr/ppermute | solution.py:39
  110.2 5.0 all-to-all-start
  118.4 27.7 %all-to-all-done = bf16[16,9,2560]{2,1,0:T(8,128)(2,1)S(1)} async-done(((bf16[16,9,2560]{2,1,0:T(8,128)(2,1)}), bf16[16,9,2560]{2,1,0:T(8,128)(2,1)S(1)}, u32[]{:S(2)}, u32[]{:S(2)}) %all-to-all-start) | async-done | bytes 737312 | tf_op jit(solution)/shard_map/while/body/eval_jaxpr/all_to_all | solution.py:123
  146.0 8.6 %conditional.3 = (bf16[16,1,9,2560]{3,2,0,1:T(8,128)(2,1)S(1)}) conditional(s32[]{:T(128)} %convert_element_type.207, () %tuple.88, (bf16[2,1,1,2560,768]{4,3,2,1,0:T(8,128)(2,1)}, s32[]{:T(128)}, bf16[16,9,2560]{2,1,0:T(8,128)(2,1)S(1)}, bf16[2,1,1,2560,768]{4,3,2,1,0:T(8,128)(2,1)}, bf16[2,1,1,768,2560]{4,3,2,1,0:T(8,128)(2,1)}) %tuple.89), branch_computations={%region_8.8_spmd, %region_9.9_spmd} | conditional | flops 1699725312 | bytes 17843720 | solution.py:124
  149.2 5.1 %fusion.11 = bf16[144,2560]{1,0:T(8,128)(2,1)S(1)} fusion(bf16[2,1,1,768,2560]{4,3,2,1,0:T(8,128)(2,1)} %get-tuple-element.444, s32[]{:T(128)} %get-tuple-element.441, bf16[144,2560]{1,0:T(8,128)(2,1)S(1)} %reshape.248, bf16[2,1,1,2560,768]{4,3,2,1,0:T(8,128)(2,1)} %get-tuple-element.443, f32[144,768]{1,0:T(8,128)S(1)} %fusion.14), kind=kOutput, calls=%fused_computation.11 | convolution fusion | flops 1133494272 | bytes 9782272 | tf_op jit(solution)/shard_map/while/body/eval_jaxpr/cond/branch_1_fun/dot_general | solution.py:76
  198.4 4.4 collective-permute-done.16
  210.9 5.0 all-to-all-start
  219.0 27.7 %all-to-all-done = bf16[16,9,2560]{2,1,0:T(8,128)(2,1)S(1)} async-done(((bf16[16,9,2560]{2,1,0:T(8,128)(2,1)}), bf16[16,9,2560]{2,1,0:T(8,128)(2,1)S(1)}, u32[]{:S(2)}, u32[]{:S(2)}) %all-to-all-start) | async-done | bytes 737312 | tf_op jit(solution)/shard_map/while/body/eval_jaxpr/all_to_all | solution.py:123
  246.7 8.6 %conditional.3 = (bf16[16,1,9,2560]{3,2,0,1:T(8,128)(2,1)S(1)}) conditional(s32[]{:T(128)} %convert_element_type.207, () %tuple.88, (bf16[2,1,1,2560,768]{4,3,2,1,0:T(8,128)(2,1)}, s32[]{:T(128)}, bf16[16,9,2560]{2,1,0:T(8,128)(2,1)S(1)}, bf16[2,1,1,2560,768]{4,3,2,1,0:T(8,128)(2,1)}, bf16[2,1,1,768,2560]{4,3,2,1,0:T(8,128)(2,1)}) %tuple.89), branch_computations={%region_8.8_spmd, %region_9.9_spmd} | conditional | flops 1699725312 | bytes 17843720 | solution.py:124
  249.9 5.1 %fusion.11 = bf16[144,2560]{1,0:T(8,128)(2,1)S(1)} fusion(bf16[2,1,1,768,2560]{4,3,2,1,0:T(8,128)(2,1)} %get-tuple-element.444, s32[]{:T(128)} %get-tuple-element.441, bf16[144,2560]{1,0:T(8,128)(2,1)S(1)} %reshape.248, bf16[2,1,1,2560,768]{4,3,2,1,0:T(8,128)(2,1)} %get-tuple-element.443, f32[144,768]{1,0:T(8,128)S(1)} %fusion.14), kind=kOutput, calls=%fused_computation.11 | convolution fusion | flops 1133494272 | bytes 9782272 | tf_op jit(solution)/shard_map/while/body/eval_jaxpr/cond/branch_1_fun/dot_general | solution.py:76
  299.1 4.5 collective-permute-done.16
  311.5 5.0 all-to-all-start
  319.7 27.7 %all-to-all-done = bf16[16,9,2560]{2,1,0:T(8,128)(2,1)S(1)} async-done(((bf16[16,9,2560]{2,1,0:T(8,128)(2,1)}), bf16[16,9,2560]{2,1,0:T(8,128)(2,1)S(1)}, u32[]{:S(2)}, u32[]{:S(2)}) %all-to-all-start) | async-done | bytes 737312 | tf_op jit(solution)/shard_map/while/body/eval_jaxpr/all_to_all | solution.py:123
  347.4 8.6 %conditional.3 = (bf16[16,1,9,2560]{3,2,0,1:T(8,128)(2,1)S(1)}) conditional(s32[]{:T(128)} %convert_element_type.207, () %tuple.88, (bf16[2,1,1,2560,768]{4,3,2,1,0:T(8,128)(2,1)}, s32[]{:T(128)}, bf16[16,9,2560]{2,1,0:T(8,128)(2,1)S(1)}, bf16[2,1,1,2560,768]{4,3,2,1,0:T(8,128)(2,1)}, bf16[2,1,1,768,2560]{4,3,2,1,0:T(8,128)(2,1)}) %tuple.89), branch_computations={%region_8.8_spmd, %region_9.9_spmd} | conditional | flops 1699725312 | bytes 17843720 | solution.py:124
  350.5 5.1 %fusion.11 = bf16[144,2560]{1,0:T(8,128)(2,1)S(1)} fusion(bf16[2,1,1,768,2560]{4,3,2,1,0:T(8,128)(2,1)} %get-tuple-element.444, s32[]{:T(128)} %get-tuple-element.441, bf16[144,2560]{1,0:T(8,128)(2,1)S(1)} %reshape.248, bf16[2,1,1,2560,768]{4,3,2,1,0:T(8,128)(2,1)} %get-tuple-element.443, f32[144,768]{1,0:T(8,128)S(1)} %fusion.14), kind=kOutput, calls=%fused_computation.11 | convolution fusion | flops 1133494272 | bytes 9782272 | tf_op jit(solution)/shard_map/while/body/eval_jaxpr/cond/branch_1_fun/dot_general | solution.py:76
  398.8 4.5 collective-permute-done.16
  411.3 5.0 all-to-all-start
  419.5 27.7 %all-to-all-done = bf16[16,9,2560]{2,1,0:T(8,128)(2,1)S(1)} async-done(((bf16[16,9,2560]{2,1,0:T(8,128)(2,1)}), bf16[16,9,2560]{2,1,0:T(8,128)(2,1)S(1)}, u32[]{:S(2)}, u32[]{:S(2)}) %all-to-all-start) | async-done | bytes 737312 | tf_op jit(solution)/shard_map/while/body/eval_jaxpr/all_to_all | solution.py:123
  447.1 8.6 %conditional.3 = (bf16[16,1,9,2560]{3,2,0,1:T(8,128)(2,1)S(1)}) conditional(s32[]{:T(128)} %convert_element_type.207, () %tuple.88, (bf16[2,1,1,2560,768]{4,3,2,1,0:T(8,128)(2,1)}, s32[]{:T(128)}, bf16[16,9,2560]{2,1,0:T(8,128)(2,1)S(1)}, bf16[2,1,1,2560,768]{4,3,2,1,0:T(8,128)(2,1)}, bf16[2,1,1,768,2560]{4,3,2,1,0:T(8,128)(2,1)}) %tuple.89), branch_computations={%region_8.8_spmd, %region_9.9_spmd} | conditional | flops 1699725312 | bytes 17843720 | solution.py:124
  450.3 5.1 %fusion.11 = bf16[144,2560]{1,0:T(8,128)(2,1)S(1)} fusion(bf16[2,1,1,768,2560]{4,3,2,1,0:T(8,128)(2,1)} %get-tuple-element.444, s32[]{:T(128)} %get-tuple-element.441, bf16[144,2560]{1,0:T(8,128)(2,1)S(1)} %reshape.248, bf16[2,1,1,2560,768]{4,3,2,1,0:T(8,128)(2,1)} %get-tuple-element.443, f32[144,768]{1,0:T(8,128)S(1)} %fusion.14), kind=kOutput, calls=%fused_computation.11 | convolution fusion | flops 1133494272 | bytes 9782272 | tf_op jit(solution)/shard_map/while/body/eval_jaxpr/cond/branch_1_fun/dot_general | solution.py:76
  498.6 4.5 collective-permute-done.16
  (429 shorter events, 292.6 us)
Async XLA Ops:
  2.4 95.6 %collective-permute-start.17 = (bf16[16,2560]{1,0:T(8,128)(2,1)S(1)}, bf16[16,2560]{1,0:T(8,128)(2,1)}, u32[]{:S(2)}, u32[]{:S(2)}) collective-permute-start(bf16[16,2560]{1,0:T(8,128)(2,1)S(1)} %copy.58), channel_id=1, source_target_pairs={{16,0},{17,1},{18,2},{19,3},{20,4},{21,5},{22,6},{23,7},{24,8},{25... | collective-permute-start | bytes 245768 | tf_op jit(solution)/shard_map/while/body/eval_jaxpr/ppermute | solution.py:45
  9.8 37.1 %all-to-all-start = ((bf16[16,9,2560]{2,1,0:T(8,128)(2,1)}), bf16[16,9,2560]{2,1,0:T(8,128)(2,1)S(1)}, u32[]{:S(2)}, u32[]{:S(2)}) async-start(bf16[16,9,2560]{2,1,0:T(8,128)(2,1)} %reshape.280), calls=%async_computation | async-start | bytes 2621440 | tf_op jit(solution)/shard_map/while/body/eval_jaxpr/all_to_all | solution.py:123
  16.7 72.9 %collective-permute-start = (bf16[16,2560]{1,0:T(8,128)(2,1)}, bf16[16,2560]{1,0:T(8,128)(2,1)}, u32[]{:S(2)}, u32[]{:S(2)}) collective-permute-start(bf16[16,2560]{1,0:T(8,128)(2,1)} %broadcast_select_fusion.6), channel_id=1, source_target_pairs={{16,0},{17,1},{18,2},{19,3},{20,4},{21,5},{22,6},{23,7},{24,8},{25... | collective-permute-start | bytes 245768 | tf_op jit(solution)/shard_map/while/body/eval_jaxpr/ppermute | solution.py:45
  70.9 13.8 %collective-permute-start.13 = (bf16[1,9,2560]{2,1,0:T(8,128)(2,1)S(1)}, bf16[1,9,2560]{2,1,0:T(8,128)(2,1)S(1)}, u32[]{:S(2)}, u32[]{:S(2)}) collective-permute-start(bf16[1,9,2560]{2,1,0:T(8,128)(2,1)S(1)} %get-tuple-element.720), channel_id=1, source_target_pairs={{0,13},{1,12},{2,15},{3,14},{4,9},{5,8},{6,11},{7,10},{8,5},{9,4},... | collective-permute-start | bytes 138248 | tf_op jit(solution)/shard_map/while/body/eval_jaxpr/ppermute | solution.py:31
  74.1 13.2 %collective-permute-start.14 = (bf16[1,9,2560]{2,1,0:T(8,128)(2,1)S(1)}, bf16[1,9,2560]{2,1,0:T(8,128)(2,1)S(1)}, u32[]{:S(2)}, u32[]{:S(2)}) collective-permute-start(bf16[1,9,2560]{2,1,0:T(8,128)(2,1)S(1)} %get-tuple-element.721), channel_id=1, source_target_pairs={{0,14},{1,15},{2,12},{3,13},{4,10},{5,11},{6,8},{7,9},{8,6},{9,7},... | collective-permute-start | bytes 138248 | tf_op jit(solution)/shard_map/while/body/eval_jaxpr/ppermute | solution.py:31
  101.6 96.8 %collective-permute-start.17 = (bf16[16,2560]{1,0:T(8,128)(2,1)S(1)}, bf16[16,2560]{1,0:T(8,128)(2,1)}, u32[]{:S(2)}, u32[]{:S(2)}) collective-permute-start(bf16[16,2560]{1,0:T(8,128)(2,1)S(1)} %copy.58), channel_id=1, source_target_pairs={{16,0},{17,1},{18,2},{19,3},{20,4},{21,5},{22,6},{23,7},{24,8},{25... | collective-permute-start | bytes 245768 | tf_op jit(solution)/shard_map/while/body/eval_jaxpr/ppermute | solution.py:45
  110.2 35.8 %all-to-all-start = ((bf16[16,9,2560]{2,1,0:T(8,128)(2,1)}), bf16[16,9,2560]{2,1,0:T(8,128)(2,1)S(1)}, u32[]{:S(2)}, u32[]{:S(2)}) async-start(bf16[16,9,2560]{2,1,0:T(8,128)(2,1)} %reshape.280), calls=%async_computation | async-start | bytes 2621440 | tf_op jit(solution)/shard_map/while/body/eval_jaxpr/all_to_all | solution.py:123
  115.9 81.3 %collective-permute-start = (bf16[16,2560]{1,0:T(8,128)(2,1)}, bf16[16,2560]{1,0:T(8,128)(2,1)}, u32[]{:S(2)}, u32[]{:S(2)}) collective-permute-start(bf16[16,2560]{1,0:T(8,128)(2,1)} %broadcast_select_fusion.6), channel_id=1, source_target_pairs={{16,0},{17,1},{18,2},{19,3},{20,4},{21,5},{22,6},{23,7},{24,8},{25... | collective-permute-start | bytes 245768 | tf_op jit(solution)/shard_map/while/body/eval_jaxpr/ppermute | solution.py:45
  178.5 13.8 %collective-permute-start.13 = (bf16[1,9,2560]{2,1,0:T(8,128)(2,1)S(1)}, bf16[1,9,2560]{2,1,0:T(8,128)(2,1)S(1)}, u32[]{:S(2)}, u32[]{:S(2)}) collective-permute-start(bf16[1,9,2560]{2,1,0:T(8,128)(2,1)S(1)} %get-tuple-element.720), channel_id=1, source_target_pairs={{0,13},{1,12},{2,15},{3,14},{4,9},{5,8},{6,11},{7,10},{8,5},{9,4},... | collective-permute-start | bytes 138248 | tf_op jit(solution)/shard_map/while/body/eval_jaxpr/ppermute | solution.py:31
  203.8 95.3 %collective-permute-start.17 = (bf16[16,2560]{1,0:T(8,128)(2,1)S(1)}, bf16[16,2560]{1,0:T(8,128)(2,1)}, u32[]{:S(2)}, u32[]{:S(2)}) collective-permute-start(bf16[16,2560]{1,0:T(8,128)(2,1)S(1)} %copy.58), channel_id=1, source_target_pairs={{16,0},{17,1},{18,2},{19,3},{20,4},{21,5},{22,6},{23,7},{24,8},{25... | collective-permute-start | bytes 245768 | tf_op jit(solution)/shard_map/while/body/eval_jaxpr/ppermute | solution.py:45
  210.9 35.8 %all-to-all-start = ((bf16[16,9,2560]{2,1,0:T(8,128)(2,1)}), bf16[16,9,2560]{2,1,0:T(8,128)(2,1)S(1)}, u32[]{:S(2)}, u32[]{:S(2)}) async-start(bf16[16,9,2560]{2,1,0:T(8,128)(2,1)} %reshape.280), calls=%async_computation | async-start | bytes 2621440 | tf_op jit(solution)/shard_map/while/body/eval_jaxpr/all_to_all | solution.py:123
  216.5 81.3 %collective-permute-start = (bf16[16,2560]{1,0:T(8,128)(2,1)}, bf16[16,2560]{1,0:T(8,128)(2,1)}, u32[]{:S(2)}, u32[]{:S(2)}) collective-permute-start(bf16[16,2560]{1,0:T(8,128)(2,1)} %broadcast_select_fusion.6), channel_id=1, source_target_pairs={{16,0},{17,1},{18,2},{19,3},{20,4},{21,5},{22,6},{23,7},{24,8},{25... | collective-permute-start | bytes 245768 | tf_op jit(solution)/shard_map/while/body/eval_jaxpr/ppermute | solution.py:45
  279.1 13.8 %collective-permute-start.13 = (bf16[1,9,2560]{2,1,0:T(8,128)(2,1)S(1)}, bf16[1,9,2560]{2,1,0:T(8,128)(2,1)S(1)}, u32[]{:S(2)}, u32[]{:S(2)}) collective-permute-start(bf16[1,9,2560]{2,1,0:T(8,128)(2,1)S(1)} %get-tuple-element.720), channel_id=1, source_target_pairs={{0,13},{1,12},{2,15},{3,14},{4,9},{5,8},{6,11},{7,10},{8,5},{9,4},... | collective-permute-start | bytes 138248 | tf_op jit(solution)/shard_map/while/body/eval_jaxpr/ppermute | solution.py:31
  282.4 13.2 %collective-permute-start.14 = (bf16[1,9,2560]{2,1,0:T(8,128)(2,1)S(1)}, bf16[1,9,2560]{2,1,0:T(8,128)(2,1)S(1)}, u32[]{:S(2)}, u32[]{:S(2)}) collective-permute-start(bf16[1,9,2560]{2,1,0:T(8,128)(2,1)S(1)} %get-tuple-element.721), channel_id=1, source_target_pairs={{0,14},{1,15},{2,12},{3,13},{4,10},{5,11},{6,8},{7,9},{8,6},{9,7},... | collective-permute-start | bytes 138248 | tf_op jit(solution)/shard_map/while/body/eval_jaxpr/ppermute | solution.py:31
  304.4 94.4 %collective-permute-start.17 = (bf16[16,2560]{1,0:T(8,128)(2,1)S(1)}, bf16[16,2560]{1,0:T(8,128)(2,1)}, u32[]{:S(2)}, u32[]{:S(2)}) collective-permute-start(bf16[16,2560]{1,0:T(8,128)(2,1)S(1)} %copy.58), channel_id=1, source_target_pairs={{16,0},{17,1},{18,2},{19,3},{20,4},{21,5},{22,6},{23,7},{24,8},{25... | collective-permute-start | bytes 245768 | tf_op jit(solution)/shard_map/while/body/eval_jaxpr/ppermute | solution.py:45
  311.5 35.8 %all-to-all-start = ((bf16[16,9,2560]{2,1,0:T(8,128)(2,1)}), bf16[16,9,2560]{2,1,0:T(8,128)(2,1)S(1)}, u32[]{:S(2)}, u32[]{:S(2)}) async-start(bf16[16,9,2560]{2,1,0:T(8,128)(2,1)} %reshape.280), calls=%async_computation | async-start | bytes 2621440 | tf_op jit(solution)/shard_map/while/body/eval_jaxpr/all_to_all | solution.py:123
  317.2 81.3 %collective-permute-start = (bf16[16,2560]{1,0:T(8,128)(2,1)}, bf16[16,2560]{1,0:T(8,128)(2,1)}, u32[]{:S(2)}, u32[]{:S(2)}) collective-permute-start(bf16[16,2560]{1,0:T(8,128)(2,1)} %broadcast_select_fusion.6), channel_id=1, source_target_pairs={{16,0},{17,1},{18,2},{19,3},{20,4},{21,5},{22,6},{23,7},{24,8},{25... | collective-permute-start | bytes 245768 | tf_op jit(solution)/shard_map/while/body/eval_jaxpr/ppermute | solution.py:45
  379.8 13.8 %collective-permute-start.13 = (bf16[1,9,2560]{2,1,0:T(8,128)(2,1)S(1)}, bf16[1,9,2560]{2,1,0:T(8,128)(2,1)S(1)}, u32[]{:S(2)}, u32[]{:S(2)}) collective-permute-start(bf16[1,9,2560]{2,1,0:T(8,128)(2,1)S(1)} %get-tuple-element.720), channel_id=1, source_target_pairs={{0,13},{1,12},{2,15},{3,14},{4,9},{5,8},{6,11},{7,10},{8,5},{9,4},... | collective-permute-start | bytes 138248 | tf_op jit(solution)/shard_map/while/body/eval_jaxpr/ppermute | solution.py:31
  383.0 13.2 %collective-permute-start.14 = (bf16[1,9,2560]{2,1,0:T(8,128)(2,1)S(1)}, bf16[1,9,2560]{2,1,0:T(8,128)(2,1)S(1)}, u32[]{:S(2)}, u32[]{:S(2)}) collective-permute-start(bf16[1,9,2560]{2,1,0:T(8,128)(2,1)S(1)} %get-tuple-element.721), channel_id=1, source_target_pairs={{0,14},{1,15},{2,12},{3,13},{4,10},{5,11},{6,8},{7,9},{8,6},{9,7},... | collective-permute-start | bytes 138248 | tf_op jit(solution)/shard_map/while/body/eval_jaxpr/ppermute | solution.py:31
  404.2 94.4 %collective-permute-start.17 = (bf16[16,2560]{1,0:T(8,128)(2,1)S(1)}, bf16[16,2560]{1,0:T(8,128)(2,1)}, u32[]{:S(2)}, u32[]{:S(2)}) collective-permute-start(bf16[16,2560]{1,0:T(8,128)(2,1)S(1)} %copy.58), channel_id=1, source_target_pairs={{16,0},{17,1},{18,2},{19,3},{20,4},{21,5},{22,6},{23,7},{24,8},{25... | collective-permute-start | bytes 245768 | tf_op jit(solution)/shard_map/while/body/eval_jaxpr/ppermute | solution.py:45
  411.3 35.8 %all-to-all-start = ((bf16[16,9,2560]{2,1,0:T(8,128)(2,1)}), bf16[16,9,2560]{2,1,0:T(8,128)(2,1)S(1)}, u32[]{:S(2)}, u32[]{:S(2)}) async-start(bf16[16,9,2560]{2,1,0:T(8,128)(2,1)} %reshape.280), calls=%async_computation | async-start | bytes 2621440 | tf_op jit(solution)/shard_map/while/body/eval_jaxpr/all_to_all | solution.py:123
  417.0 81.3 %collective-permute-start = (bf16[16,2560]{1,0:T(8,128)(2,1)}, bf16[16,2560]{1,0:T(8,128)(2,1)}, u32[]{:S(2)}, u32[]{:S(2)}) collective-permute-start(bf16[16,2560]{1,0:T(8,128)(2,1)} %broadcast_select_fusion.6), channel_id=1, source_target_pairs={{16,0},{17,1},{18,2},{19,3},{20,4},{21,5},{22,6},{23,7},{24,8},{25... | collective-permute-start | bytes 245768 | tf_op jit(solution)/shard_map/while/body/eval_jaxpr/ppermute | solution.py:45
  479.6 13.8 %collective-permute-start.13 = (bf16[1,9,2560]{2,1,0:T(8,128)(2,1)S(1)}, bf16[1,9,2560]{2,1,0:T(8,128)(2,1)S(1)}, u32[]{:S(2)}, u32[]{:S(2)}) collective-permute-start(bf16[1,9,2560]{2,1,0:T(8,128)(2,1)S(1)} %get-tuple-element.720), channel_id=1, source_target_pairs={{0,13},{1,12},{2,15},{3,14},{4,9},{5,8},{6,11},{7,10},{8,5},{9,4},... | collective-permute-start | bytes 138248 | tf_op jit(solution)/shard_map/while/body/eval_jaxpr/ppermute | solution.py:31
  482.8 13.2 %collective-permute-start.14 = (bf16[1,9,2560]{2,1,0:T(8,128)(2,1)S(1)}, bf16[1,9,2560]{2,1,0:T(8,128)(2,1)S(1)}, u32[]{:S(2)}, u32[]{:S(2)}) collective-permute-start(bf16[1,9,2560]{2,1,0:T(8,128)(2,1)S(1)} %get-tuple-element.721), channel_id=1, source_target_pairs={{0,14},{1,15},{2,12},{3,13},{4,10},{5,11},{6,8},{7,9},{8,6},{9,7},... | collective-permute-start | bytes 138248 | tf_op jit(solution)/shard_map/while/body/eval_jaxpr/ppermute | solution.py:31
  (77 other events, 528.7 us)
